TPU v7x, 256 devices: a whole 4x4x8 slice. The times are simulated.
256 devices in a mesh: shard: 32 (over x, z_hi, y), rep: 8 (over z_lo, core).
Axes of the slice: x: 4, y: 4, z: 8 (z_hi: 2, z_lo: 4; z = z_hi * 4 + z_lo), core: 2. Of those that a mesh axis runs over, the one named last changes fastest.
Arguments:
- momentum: bfloat16 [32, 512, 2048], P(None, 'shard'), may hold values from -6 to 6
- gradient: bfloat16 [32, 512, 2048], P(None, 'shard'), may hold values from -6 to 6
Outputs:
- new_momentum: bfloat16 [32, 512, 2048], P(None, 'shard')
- update: bfloat16 [32, 512, 2048], P(None, 'shard')
All inputs are finite; a program needn't handle non-finite values.
Results may differ from a plain program's by a relative error of at most 0.00065.
The roundings to bfloat16 on the way count: a program that leaves them out, or rounds other values in their place, can miss the bound.
Values may be sent and summed in bfloat16 or wider, within the bound.
A program may use at most 64 MiB of HBM per device.

v0:
```python
import jax
import jax.numpy as jnp
from jax import lax
from jax.sharding import PartitionSpec as P

ROWS = 512
COLS = 2048
ITERS = 5


coef_a = 3.4445
coef_b = -4.775
coef_c = 2.0315


def gram_sum(values):
    local_gram = jnp.dot(
        values, values.T, precision=lax.Precision.HIGHEST, preferred_element_type=jnp.float32
    )
    return lax.psum(local_gram, "rep")


def newton_step(gram_matrix, iterate):
    polynomial = coef_b * gram_matrix + coef_c * jnp.dot(
        gram_matrix, gram_matrix, precision=lax.Precision.HIGHEST
    )
    return coef_a * iterate + jnp.dot(polynomial, iterate, precision=lax.Precision.HIGHEST)


def shards(momentum, gradient):
    new_momentum = (0.95 * momentum.astype(jnp.float32) + gradient.astype(jnp.float32)).astype(
        jnp.bfloat16
    )
    blended = (gradient.astype(jnp.float32) + 0.95 * new_momentum.astype(jnp.float32)).astype(
        jnp.bfloat16
    )
    col_width = blended.shape[2] // lax.axis_size("rep")
    col_start = lax.axis_index("rep") * col_width
    col_block = lax.dynamic_slice_in_dim(blended, col_start, col_width, 2)
    regrouped = lax.all_to_all(col_block, "shard", split_axis=0, concat_axis=1, tiled=True)
    scale_value = jnp.sqrt(jnp.float32(max(ROWS, COLS)))
    columns_block = regrouped[0].astype(jnp.float32)
    square_total = lax.psum(jnp.sum(columns_block * columns_block), "rep")
    norm_value = jnp.sqrt(square_total) + 1e-07
    iterate = columns_block / norm_value
    gram_matrix = gram_sum(iterate)
    for sweep in range(ITERS):
        if sweep > 0:
            gram_matrix = gram_sum(iterate)
        iterate = newton_step(gram_matrix, iterate)
    result = (iterate * scale_value).astype(jnp.bfloat16)[None]
    full_matrix = lax.all_gather(result, "rep", axis=2, tiled=True)
    update = lax.all_to_all(full_matrix, "shard", split_axis=1, concat_axis=0, tiled=True)
    return (new_momentum, update)


def solution(mesh):
    return jax.shard_map(
        shards,
        mesh=mesh,
        in_specs=(P(None, "shard", None), P(None, "shard", None)),
        out_specs=(P(None, "shard", None), P(None, "shard", None)),
        check_vma=False,
    )
```

profile of v0, /device:TPU:1, one launch (start us, length us, event | category | flops | bytes accessed | tf_op | source)
XLA Modules:
  0.0 596.6 jit_solution(5018397277071204557)
XLA Ops:
  7.2 0.0 all-reduce.6.cloned.1.call-start
  7.2 4.2 convert_element_type.28
  11.4 1.0 add_convert_fusion
  12.4 0.0 copy-start.1
  12.4 1.6 fusion.8
  14.0 26.4 %all_to_all.21 = bf16[32,16,256]{2,1,0:T(8,128)(2,1)S(1)} all-to-all(bf16[32,16,256]{2,1,0:T(8,128)(2,1)S(1)} %fusion.8), channel_id=1, replica_groups=mesh['shard'=32,'rep'=8] {'shard'}, dimensions={0} | all-to-all | bytes 524288 | tf_op jit(solution)/shard_map/all_to_all | solution.py:40
  40.4 0.7 fusion.7
  41.1 15.6 %psum.42 = f32[]{:T(128)} all-reduce(f32[]{:T(128)} %fusion.7), channel_id=1, replica_groups=mesh['shard'=32,'rep'=8] {'rep'}, use_global_device_ids=true, to_apply=%region_1.0 | all-reduce | flops 1 | bytes 8 | tf_op jit(solution)/shard_map/psum | solution.py:43
  57.4 0.1 convert_divide_fusion
  57.5 2.0 fusion.9
  59.5 0.0 all-reduce.6.cloned.1.call-update
  59.5 0.0 all-reduce.8.cloned.1.call-start
  59.6 64.8 %all-reduce.6.cloned.1.call-done = f32[512,512]{1,0:T(8,128)} async-done(((f32[512,512]{1,0:T(8,128)}), f32[512,512]{1,0:T(8,128)}) %all-reduce.6.cloned.1.call-update) | async-done | bytes 1048592 | tf_op jit(solution)/shard_map/psum | solution.py:20
  124.4 3.9 fusion.4
  128.4 1.0 convolution_add_fusion.4
  129.4 2.0 fusion.10
  131.4 0.0 all-reduce.8.cloned.1.call-update
  131.4 0.0 all-reduce.10.cloned.1.call-start
  131.4 73.5 %all-reduce.8.cloned.1.call-done = f32[512,512]{1,0:T(8,128)} async-done(((f32[512,512]{1,0:T(8,128)}), f32[512,512]{1,0:T(8,128)}) %all-reduce.8.cloned.1.call-update) | async-done | bytes 1048592 | tf_op jit(solution)/shard_map/psum | solution.py:20
  204.9 3.9 fusion.3
  208.8 1.0 convolution_add_fusion.3
  209.8 2.0 fusion.11
  211.8 0.0 all-reduce.10.cloned.1.call-update
  211.8 0.2 all-reduce.12.cloned.1.call-start
  212.1 73.3 %all-reduce.10.cloned.1.call-done = f32[512,512]{1,0:T(8,128)} async-done(((f32[512,512]{1,0:T(8,128)}), f32[512,512]{1,0:T(8,128)}) %all-reduce.10.cloned.1.call-update) | async-done | bytes 1048592 | tf_op jit(solution)/shard_map/psum | solution.py:20
  285.4 3.9 fusion.2
  289.3 1.0 convolution_add_fusion.2
  290.3 2.0 fusion.12
  292.3 0.0 all-reduce.12.cloned.1.call-update
  292.3 0.0 all-reduce.14.cloned.1.call-start
  292.4 73.5 %all-reduce.12.cloned.1.call-done = f32[512,512]{1,0:T(8,128)} async-done(((f32[512,512]{1,0:T(8,128)}), f32[512,512]{1,0:T(8,128)}) %all-reduce.12.cloned.1.call-update) | async-done | bytes 1048592 | tf_op jit(solution)/shard_map/psum | solution.py:20
  365.9 3.9 fusion.1
  369.8 1.0 convolution_add_fusion.1
  370.8 2.0 fusion.13
  372.8 0.0 all-reduce.14.cloned.1.call-update
  372.8 0.3 all-gather.3.cloned.1.call-start
  373.1 73.2 %all-reduce.14.cloned.1.call-done = f32[512,512]{1,0:T(8,128)} async-done(((f32[512,512]{1,0:T(8,128)}), f32[512,512]{1,0:T(8,128)}) %all-reduce.14.cloned.1.call-update) | async-done | bytes 1048592 | tf_op jit(solution)/shard_map/psum | solution.py:20
  446.3 3.9 fusion
  450.3 1.7 fusion.6
  452.0 0.0 all-gather.3.cloned.1.call-update
  452.0 40.6 %all-gather.3.cloned.1.call-done = bf16[512,2048]{1,0:T(8,128)(2,1)} async-done(((bf16[512,256]{1,0:T(8,128)(2,1)}), bf16[512,2048]{1,0:T(8,128)(2,1)}) %all-gather.3.cloned.1.call-update) | async-done | bytes 2097168 | tf_op jit(solution)/shard_map/all_gather | solution.py:52
  492.6 6.7 %copy.8 = bf16[1,512,2048]{2,0,1:T(2,128)(2,1)} copy(bf16[1,512,2048]{2,1,0:T(8,128)(2,1)} %bitcast.41) | data formatting | bytes 4194304 | tf_op jit(solution)/shard_map/all_gather | solution.py:52
  499.3 0.5 broadcast.39
  499.9 13.2 %reduce.3 = bf16[512,2048]{1,0:T(8,128)(2,1)S(1)} reduce(bf16[512,1,2048]{2,1,0:T(2,128)(2,1)} %bitcast.37, bf16[]{:T(256)} %broadcast.39), dimensions={1}, to_apply=%bitcast.36.reduce_sub_computation | reduce | bytes 4194306
  513.0 2.8 reshape.22
  515.8 62.4 %all_to_all.22 = bf16[32,2,16384]{2,1,0:T(2,128)(2,1)S(1)} all-to-all(bf16[32,2,16384]{2,1,0:T(2,128)(2,1)} %reshape.22), channel_id=1, replica_groups=mesh['shard'=32,'rep'=8] {'shard'}, dimensions={0} | all-to-all | bytes 4194304 | tf_op jit(solution)/shard_map/all_to_all | solution.py:53
  578.2 6.8 %reshape.23 = bf16[512,1,2048]{2,1,0:T(2,128)(2,1)} reshape(bf16[32,2,16384]{2,1,0:T(2,128)(2,1)S(1)} %all_to_all.22) | data formatting | bytes 4194304
  585.0 4.8 copy.6
  (5 shorter events, 0.0 us)
Async XLA Ops:
  7.2 117.3 %all-reduce.6.cloned.1.call-start = ((), (), s32[]{:S(2)}) async-start(), calls=%async_computation.2 | async-start | bytes 2097152 | tf_op jit(solution)/shard_map/psum | solution.py:20
  7.2 4.2 copy-start
  7.2 4.2 copy-start.2
  12.4 45.0 %copy-start.1 = (bf16[32,16,2048]{2,1,0:T(8,128)(2,1)}, bf16[32,16,2048]{2,1,0:T(8,128)(2,1)S(1)}, u32[]{:S(2)}) copy-start(bf16[32,16,2048]{2,1,0:T(8,128)(2,1)S(1)} %add_convert_fusion) | copy-start | bytes 6291460
  59.5 145.3 %all-reduce.8.cloned.1.call-start = ((), (), s32[]{:S(2)}) async-start(), calls=%async_computation.3 | async-start | bytes 2097152 | tf_op jit(solution)/shard_map/psum | solution.py:20
  131.4 154.0 %all-reduce.10.cloned.1.call-start = ((), (), s32[]{:S(2)}) async-start(), calls=%async_computation.4 | async-start | bytes 2097152 | tf_op jit(solution)/shard_map/psum | solution.py:20
  211.8 154.0 %all-reduce.12.cloned.1.call-start = ((), (), s32[]{:S(2)}) async-start(), calls=%async_computation.5 | async-start | bytes 2097152 | tf_op jit(solution)/shard_map/psum | solution.py:20
  292.3 154.0 %all-reduce.14.cloned.1.call-start = ((), (), s32[]{:S(2)}) async-start(), calls=%async_computation.6 | async-start | bytes 2097152 | tf_op jit(solution)/shard_map/psum | solution.py:20
  372.8 119.8 %all-gather.3.cloned.1.call-start = ((), (), s32[]{:S(2)}) async-start(), calls=%async_computation.7 | async-start | bytes 2359296 | tf_op jit(solution)/shard_map/all_gather | solution.py:52
Sparse Core Ops, SparseCore 0:
  59.7 64.7 all-reduce.5
  131.5 73.3 all-reduce.7
  212.0 73.3 all-reduce.9
  292.4 73.3 all-reduce.11
  373.0 73.3 all-reduce.13
  452.1 40.4 all-gather.2
where the time goes:
time: 597 us
  waiting for transfers between devices  399 us (67%)
  blocking collectives  104 us (17%)
  matrix products  35.3 us (6%)
  local copies, waits for them, and re-layouts  21.6 us (4%)
  other arithmetic  20.7 us (3%)
  between operations  14.9 us (2%)
    psum x5, waiting for transfers between devices, gram_sum(): return lax.psum(local_gram, 'rep')  358 us
    all_to_all x1, blocking collectives, shards(): lax.all_to_all(full_matrix, 'shard', split_axis=1, concat_axis=0, tiled=T...  62.4 us
    all_gather x1, waiting for transfers between devices, shards(): full_matrix = lax.all_gather(result, 'rep', axis=2, tiled=True)  40.6 us
    all_to_all x1, blocking collectives, shards(): lax.all_to_all(col_block, 'shard', split_axis=0, concat_axis=1, tiled=True)  26.4 us
    dot_general x5, matrix products, newton_step(): jnp.dot(gram_matrix, gram_matrix, precision=lax.Precision.HIGHEST)  19.6 us
    psum x1, blocking collectives, shards(): square_total = lax.psum(jnp.sum(columns_block * columns_block), 'rep')  15.6 us
    unnamed x10, local copies, waits for them, and re-layouts  14.8 us
    unnamed x1, other arithmetic  13.2 us
  transfers between devices with their start and end apart: 6, of which 6 were waited for; matrix products, arithmetic and copies ran while one was open for 0% of the time, Pallas kernels for 0%

commit v1 on v0

v1 whole, which is shorter than its diff:
```python
import functools

import jax
import jax.numpy as jnp
from jax import lax
from jax.experimental import pallas as pl
from jax.experimental.pallas import tpu as pltpu
from jax.sharding import PartitionSpec as P

ROWS = 512
COLS = 2048
ITERS = 5
EXPERTS = 32

coef_a = 3.4445
coef_b = -4.775
coef_c = 2.0315

MESH = pl.DeviceIdType.MESH
F32 = jnp.float32
BF16 = jnp.bfloat16

BAND = ROWS // 32
HALF = COLS // 2
QUARTER = HALF // 4
SPAN = 2
CHUNKS = 16 // SPAN
PER_X = 4 // SPAN


def hop_order(step):
    return lax.rem(step + step // 2 - 2 * (step // 3), 4)


class Place:
    def __init__(self):
        self.s = lax.axis_index("shard")
        self.r = lax.axis_index("rep")
        self.x = self.s // 8
        self.h = (self.s // 4) % 2
        self.y = self.s % 4
        self.zl = self.r // 2
        self.c = self.r % 2
        self.flow = self.zl // 2
        self.entry = 3 * (1 - self.flow)
        self.col = pl.multiple_of(self.c * HALF, HALF)
        self.other_col = pl.multiple_of((1 - self.c) * HALF, HALF)

    def shard(self, x, h, y):
        return x * 8 + h * 4 + y

    def rep(self, zl):
        return zl * 2 + self.c


def greet(p):
    barrier = pltpu.get_barrier_semaphore()

    def signal(s, r):
        pl.semaphore_signal(barrier, inc=1, device_id=(s, r), device_id_type=MESH)

    def near(i, _):
        x, y = lax.rem(p.x + i // 4, 4), lax.rem(p.y + i % 4, 4)

        @pl.when(i > 0)
        def _():
            signal(p.shard(x, p.h, y), p.r)

        return 0

    def across(i, _):
        x, y = lax.rem(p.x + i // 4, 4), lax.rem(p.y + i % 4, 4)
        first = 2 * (1 - p.zl // 3)
        signal(p.shard(x, 1 - p.h, y), p.rep(first))
        signal(p.shard(x, 1 - p.h, y), p.rep(first + 1))
        return 0

    @pl.when((p.zl == 0) | (p.zl == 3))
    def _():
        lax.fori_loop(0, 16, across, 0)

    lax.fori_loop(0, 16, near, 0)
    signal(p.s, p.zl * 2 + 1 - p.c)

    @pl.when(p.zl < 3)
    def _():
        signal(p.s, p.rep(p.zl + 1))

    @pl.when(p.zl > 0)
    def _():
        signal(p.s, p.rep(p.zl - 1))


def await_greetings(p):
    inner = (p.zl * (3 - p.zl)) // 2
    pl.semaphore_wait(pltpu.get_barrier_semaphore(), 15 + 16 + 1 + 1 + inner)


class Exchange:
    def __init__(self, p, src, dst, direct, relayed, pair_direct, pair_relayed, sends):
        self.p, self.src, self.dst = p, src, dst
        self.direct, self.relayed = direct, relayed
        self.pair_direct, self.pair_relayed = pair_direct, pair_relayed
        self.sends = sends

    def send_across(self):
        p = self.p
        cols = pl.multiple_of(p.zl * QUARTER, QUARTER)
        into = pl.multiple_of(p.c * HALF + p.zl * QUARTER, QUARTER)
        chunk = p.x * PER_X + p.y // SPAN

        def one(i, _):
            x = lax.rem(p.x + hop_order(i // 4), 4)
            y = lax.rem(p.y + hop_order(i % 4), 4)
            to = p.shard(x, 1 - p.h, y)
            pltpu.make_async_remote_copy(
                src_ref=self.src.at[to, :, pl.ds(cols, QUARTER)],
                dst_ref=self.dst.at[p.s, :, pl.ds(into, QUARTER)],
                send_sem=self.sends.at[0],
                recv_sem=self.relayed.at[p.flow, chunk],
                device_id=(to, p.rep(p.entry)),
                device_id_type=MESH,
            ).start()
            return 0

        lax.fori_loop(0, 16, one, 0)

    def send_near(self):
        p = self.p

        def one(i, _):
            x = lax.rem(p.x + hop_order(i // 4), 4)
            y = lax.rem(p.y + hop_order(i % 4), 4)
            to = p.shard(x, p.h, y)

            @pl.when(i > 0)
            def _():
                pltpu.make_async_remote_copy(
                    src_ref=self.src.at[to],
                    dst_ref=self.dst.at[p.s, :, pl.ds(p.col, HALF)],
                    send_sem=self.sends.at[1],
                    recv_sem=self.direct.at[p.x],
                    device_id=(to, p.r),
                    device_id_type=MESH,
                ).start()

            return 0

        pltpu.make_async_copy(
            self.src.at[p.s],
            self.dst.at[p.s, :, pl.ds(p.col, HALF)],
            self.direct.at[p.x],
        ).start()
        lax.fori_loop(0, 16, one, 0)

    def flow_chunk(self, flow, k, half_col):
        p = self.p
        x = lax.rem(p.x + hop_order(k // PER_X), 4)
        part = k % PER_X
        slot = p.shard(x, 1 - p.h, part * SPAN)
        cols = pl.multiple_of(half_col + flow * 2 * QUARTER, 2 * QUARTER)
        at = self.dst.at[pl.ds(slot, SPAN), :, pl.ds(cols, 2 * QUARTER)]
        return at, x * PER_X + part

    def relay(self, flow, k, sink):
        p = self.p
        at, sem = self.flow_chunk(flow, k, p.c * HALF)
        pltpu.make_async_copy(at, at, self.relayed.at[flow, sem]).wait()
        more = (p.zl > 0) if flow == 0 else (p.zl < 3)

        @pl.when(more)
        def _():
            pltpu.make_async_remote_copy(
                src_ref=at,
                dst_ref=at,
                send_sem=self.sends.at[2 + flow],
                recv_sem=self.relayed.at[flow, sem],
                device_id=(p.s, p.rep(p.zl - 1 if flow == 0 else p.zl + 1)),
                device_id_type=MESH,
            ).start()

        pltpu.make_async_remote_copy(
            src_ref=at,
            dst_ref=at,
            send_sem=self.sends.at[4],
            recv_sem=self.pair_relayed.at[flow, sem],
            device_id=(p.s, p.zl * 2 + 1 - p.c),
            device_id_type=MESH,
        ).start()
        sink(at)

    def direct_group(self, g, half_col):
        p = self.p
        x = lax.rem(p.x + hop_order(g), 4)
        cols = pl.multiple_of(half_col, HALF)
        at = self.dst.at[pl.ds(p.shard(x, p.h, 0), 4), :, pl.ds(cols, HALF)]
        return at, x

    def pass_direct(self, g, sink):
        p = self.p
        at, x = self.direct_group(g, p.c * HALF)
        pltpu.make_async_copy(at, at, self.direct.at[x]).wait()
        pltpu.make_async_remote_copy(
            src_ref=at,
            dst_ref=at,
            send_sem=self.sends.at[5],
            recv_sem=self.pair_direct.at[x],
            device_id=(p.s, p.zl * 2 + 1 - p.c),
            device_id_type=MESH,
        ).start()
        sink(at)

    def gather(self, sink):
        p = self.p

        def step(t, _):
            for flow in (0, 1):
                k = t - (3 - p.zl if flow == 0 else p.zl)

                @pl.when((k >= 0) & (k < CHUNKS))
                def _():
                    self.relay(flow, k, sink)

            @pl.when(t >= CHUNKS - 1)
            def _():
                self.pass_direct(t - (CHUNKS - 1), sink)

            return 0

        lax.fori_loop(0, CHUNKS + 3, step, 0)

        def partner_direct(g, _):
            at, x = self.direct_group(g, (1 - p.c) * HALF)
            pltpu.make_async_copy(at, at, self.pair_direct.at[x]).wait()
            sink(at)
            return 0

        lax.fori_loop(0, 4, partner_direct, 0)

        def partner_relayed(k, _):
            for flow in (0, 1):
                at, sem = self.flow_chunk(flow, k, (1 - p.c) * HALF)
                pltpu.make_async_copy(at, at, self.pair_relayed.at[flow, sem]).wait()
                sink(at)
            return 0

        lax.fori_loop(0, CHUNKS, partner_relayed, 0)

    def finish_sends(self):
        p = self.p

        def drain(index, slots):
            of = self.src.at[pl.ds(0, slots)]
            pltpu.make_async_copy(of, of, self.sends.at[index]).wait()

        drain(0, 4)
        drain(1, 15)

        @pl.when(p.zl > 0)
        def _():
            drain(2, 8)

        @pl.when(p.zl < 3)
        def _():
            drain(3, 8)

        drain(4, 16)
        drain(5, 16)


def halves(value, high_ref, low_ref):
    high = value.astype(BF16)
    high_ref[...] = high
    low_ref[...] = (value - high.astype(F32)).astype(BF16)


def mul(lh, ll, rh, rl):
    dot = functools.partial(jnp.dot, preferred_element_type=F32)
    return dot(lh[...], rh[...]) + (dot(lh[...], rl[...]) + dot(ll[...], rh[...]))


def chain(x_ref, gram, q, ah, al, rh, rl, ch, cl, qh, ql):
    eye = lax.broadcasted_iota(jnp.int32, (ROWS, ROWS), 0) == lax.broadcasted_iota(
        jnp.int32, (ROWS, ROWS), 1
    )
    values = x_ref[...].reshape(ROWS, COLS)
    raw = lax.dot_general(
        values, values, (((1,), (1,)), ((), ())), preferred_element_type=F32
    )
    gram[...] = raw
    square = jnp.sum(jnp.where(eye, raw, 0.0), axis=(0, 1), keepdims=True)
    inverse = 1.0 / (jnp.sqrt(square) + 1e-07)
    gram[...] = gram[...] * inverse * inverse
    q[...] = jnp.where(eye, 1.0, 0.0)
    halves(q[...], qh, ql)

    def sweep(i, _):
        halves(gram[...], ah, al)
        poly = coef_b * gram[...] + coef_c * mul(ah, al, ah, al)
        halves(poly, rh, rl)
        q[...] = coef_a * q[...] + mul(rh, rl, qh, ql)
        halves(q[...], qh, ql)

        @pl.when(i < ITERS - 1)
        def _():
            gram[...] = coef_a * gram[...] + mul(rh, rl, ah, al)
            halves(gram[...], ch, cl)
            gram[...] = coef_a * gram[...] + mul(ch, cl, rh, rl)

        return 0

    lax.fori_loop(0, ITERS, sweep, 0)
    return inverse * jnp.sqrt(F32(max(ROWS, COLS)))


def kernel(
    mom, grad, new_mom, update, mv, gv, nv, sb, xb, yb, ob,
    gram, q, ah, al, rh, rl, ch, cl, qh, ql,
    load_sem, store_sem, direct, relayed, pair_direct, pair_relayed, sends,
):
    p = Place()
    greet(p)

    def load(index, src, dst, col):
        return pltpu.make_async_copy(
            src.at[:, :, pl.ds(col, HALF)],
            dst.at[:, :, pl.ds(col, HALF)],
            load_sem.at[index],
        )

    loads = [
        load(0, mom, mv, p.col),
        load(1, grad, gv, p.col),
        load(2, mom, mv, p.other_col),
        load(3, grad, gv, p.other_col),
    ]
    for copy in loads:
        copy.start()
    loads[0].wait()
    loads[1].wait()

    def momentum(e, col):
        cols = pl.ds(col, HALF)
        g = gv[e, :, cols].astype(F32)
        n = (0.95 * mv[e, :, cols].astype(F32) + g).astype(BF16)
        nv[e, :, cols] = n
        return n, g

    def blend(e, _):
        n, g = momentum(e, p.col)
        sb[e] = (g + 0.95 * n.astype(F32)).astype(BF16)
        return 0

    lax.fori_loop(0, EXPERTS, blend, 0)
    await_greetings(p)

    def exchange(phase, src, dst):
        return Exchange(
            p, src, dst, direct.at[phase], relayed.at[phase],
            pair_direct.at[phase], pair_relayed.at[phase], sends.at[phase],
        )

    inward = exchange(0, sb, xb)
    inward.send_across()
    inward.send_near()

    loads[2].wait()
    loads[3].wait()

    def rest(e, _):
        momentum(e, p.other_col)
        return 0

    lax.fori_loop(0, EXPERTS, rest, 0)
    store = pltpu.make_async_copy(nv, new_mom, store_sem.at[0])
    store.start()
    inward.gather(lambda at: None)

    factor = chain(xb, gram, q, ah, al, rh, rl, ch, cl, qh, ql)

    dot = functools.partial(jnp.dot, preferred_element_type=F32)

    def product(h, cols, width):
        rows = [pl.ds(pl.multiple_of(x * 128 + h * 64, 64), 64) for x in range(4)]
        high = jnp.concatenate([qh[i, :] for i in rows], 0)
        low = jnp.concatenate([ql[i, :] for i in rows], 0)
        values = xb[:, :, pl.ds(cols, width)].reshape(ROWS, width)
        return ((dot(high, values) + dot(low, values)) * factor).astype(BF16)

    outward = exchange(1, yb, ob)
    across = pl.multiple_of(p.c * HALF + p.zl * QUARTER, QUARTER)
    part = product(1 - p.h, across, QUARTER).reshape(4, 4, BAND, QUARTER)
    for x in range(4):
        slots = pl.ds(p.shard(x, 1 - p.h, 0), 4)
        yb[slots, :, pl.ds(pl.multiple_of(p.zl * QUARTER, QUARTER), QUARTER)] = part[x]
    outward.send_across()
    part = product(p.h, p.col, HALF).reshape(4, 4, BAND, HALF)
    for x in range(4):
        yb[pl.ds(p.shard(x, p.h, 0), 4)] = part[x]
    outward.send_near()
    outward.gather(lambda at: None)
    out = pltpu.make_async_copy(ob, update, store_sem.at[1])
    out.start()
    inward.finish_sends()
    outward.finish_sends()
    store.wait()
    out.wait()


def shards(momentum, gradient):
    whole = (EXPERTS, BAND, COLS)
    dma = pltpu.SemaphoreType.DMA
    square = (ROWS, ROWS)
    return pl.pallas_call(
        kernel,
        out_shape=(
            jax.ShapeDtypeStruct(whole, BF16),
            jax.ShapeDtypeStruct(whole, BF16),
        ),
        in_specs=[pl.BlockSpec(memory_space=pl.ANY)] * 2,
        out_specs=[pl.BlockSpec(memory_space=pl.ANY)] * 2,
        scratch_shapes=[
            pltpu.VMEM(whole, BF16),
            pltpu.VMEM(whole, BF16),
            pltpu.VMEM(whole, BF16),
            pltpu.VMEM((EXPERTS, BAND, HALF), BF16),
            pltpu.VMEM(whole, BF16),
            pltpu.VMEM((EXPERTS, BAND, HALF), BF16),
            pltpu.VMEM(whole, BF16),
            pltpu.VMEM(square, F32),
            pltpu.VMEM(square, F32),
        ]
        + [pltpu.VMEM(square, BF16)] * 8
        + [
            dma((4,)),
            dma((2,)),
            dma((2, 4)),
            dma((2, 2, CHUNKS)),
            dma((2, 4)),
            dma((2, 2, CHUNKS)),
            dma((2, 6)),
        ],
        compiler_params=pltpu.CompilerParams(
            collective_id=0,
            has_side_effects=True,
            vmem_limit_bytes=48 * 1024 * 1024,
        ),
    )(momentum, gradient)


def solution(mesh):
    return jax.shard_map(
        shards,
        mesh=mesh,
        in_specs=(P(None, "shard", None), P(None, "shard", None)),
        out_specs=(P(None, "shard", None), P(None, "shard", None)),
        check_vma=False,
    )
```

time: 597 us -> 102 us (0.17)
  waiting for transfers between devices: 399 us -> 0 us
  blocking collectives: 104 us -> 0 us
  Pallas kernels: 0 us -> 98.8 us
  matrix products: 35.3 us -> 0 us
  other arithmetic: 20.7 us -> 0 us
  local copies, waits for them, and re-layouts: 21.6 us -> 2.64 us
  between operations: 14.9 us -> 0.64 us
    psum x5 -> x0, waiting for transfers between devices: 358 us -> none  [gram_sum(): return lax.psum(local_gram, 'rep')]
    pallas_call x0 -> x1, Pallas kernels: none -> 98.8 us  [shards(): pl.pallas_call(kernel, out_shape=(jax.ShapeDtypeStruct(whole, BF16), jax....]
    all_to_all x2 -> x0, blocking collectives: 88.8 us -> none  [the longest x1 62.4 us: shards(): lax.all_to_all(full_matrix, 'shard', split_axis=1, concat_axis=0, tiled=T...]
    all_gather x1 -> x0, waiting for transfers between devices: 40.6 us -> none  [shards(): full_matrix = lax.all_gather(result, 'rep', axis=2, tiled=True)]
    dot_general x15 -> x0, matrix products: 35.3 us -> none  [the longest x5 19.6 us: newton_step(): jnp.dot(gram_matrix, gram_matrix, precision=lax.Precision.HIGHEST)]
    psum x1 -> x0, blocking collectives: 15.6 us -> none  [shards(): square_total = lax.psum(jnp.sum(columns_block * columns_block), 'rep')]
    unnamed x1 -> x0, other arithmetic: 13.2 us -> none
    unnamed x10 -> x2, local copies, waits for them, and re-layouts: 14.8 us -> 2.64 us
  transfers between devices with their start and end apart: 6 -> 0, of which waited for: 6 -> 0; matrix products, arithmetic and copies ran while one was open for 0% -> 0% of each run, Pallas kernels for 0% -> 0%
where the time goes in v1:
time: 102 us
  Pallas kernels  98.8 us (97%)
  local copies, waits for them, and re-layouts  2.64 us (3%)
    pallas_call x1, Pallas kernels, shards(): pl.pallas_call(kernel, out_shape=(jax.ShapeDtypeStruct(whole, BF16), jax....  98.8 us
    unnamed x2, local copies, waits for them, and re-layouts  2.64 us

profile of v1, /device:TPU:1, one launch (start us, length us, event | category | flops | bytes accessed | tf_op | source)
XLA Modules:
  0.0 102.1 jit_solution(8823279946545180707)
XLA Ops:
  0.6 98.8 %shard_map.41 = (bf16[32,16,2048]{2,1,0:T(8,128)(2,1)S(1)}, bf16[32,16,2048]{2,1,0:T(8,128)(2,1)S(1)}) custom-call(bf16[32,16,2048]{2,1,0:T(8,128)(2,1)} %mom.1, bf16[32,16,2048]{2,1,0:T(8,128)(2,1)} %grad.1), custom_call_target="tpu_custom_call" | custom-call | tf_op jit(solution)/shard_map/pallas_call | solution.py:414
  99.5 1.3 %copy.6 = bf16[32,16,2048]{2,1,0:T(8,128)(2,1)} copy(bf16[32,16,2048]{2,1,0:T(8,128)(2,1)S(1)} %get-tuple-element.4) | data formatting | bytes 4194304
  100.8 1.3 %copy.7 = bf16[32,16,2048]{2,1,0:T(8,128)(2,1)} copy(bf16[32,16,2048]{2,1,0:T(8,128)(2,1)S(1)} %get-tuple-element.5) | data formatting | bytes 4194304

commit v2 on v1

v2 whole, which is shorter than its diff:
```python
import functools

import jax
import jax.numpy as jnp
from jax import lax
from jax.experimental import pallas as pl
from jax.experimental.pallas import tpu as pltpu
from jax.sharding import PartitionSpec as P

ROWS = 512
COLS = 2048
ITERS = 5
EXPERTS = 32

coef_a = 3.4445
coef_b = -4.775
coef_c = 2.0315

MESH = pl.DeviceIdType.MESH
F32 = jnp.float32
BF16 = jnp.bfloat16

BAND = ROWS // 32
HALF = COLS // 2
PART = COLS // 8
LAG = 4
NEAR_AT = 13


def hop_order(step):
    return lax.rem(step + step // 2 - 2 * (step // 3), 4)


class Place:
    def __init__(self):
        self.s = lax.axis_index("shard")
        self.r = lax.axis_index("rep")
        self.x = self.s // 8
        self.h = (self.s // 4) % 2
        self.y = self.s % 4
        self.zl = self.r // 2
        self.c = self.r % 2
        self.partner = self.zl * 2 + 1 - self.c
        self.hop = (1 - self.c) * (3 - self.zl) + self.c * self.zl
        self.before = self.r + 2 - 4 * self.c
        self.after = self.r - 2 + 4 * self.c
        self.first = 6 - 5 * (self.zl // 2)
        self.col = pl.multiple_of(self.c * HALF, HALF)
        self.other_col = pl.multiple_of((1 - self.c) * HALF, HALF)
        self.part = pl.multiple_of(self.r * PART, PART)

    def shard(self, x, h, y):
        return x * 8 + h * 4 + y

    def far(self, i):
        x = lax.rem(self.x + hop_order(i // 4), 4)
        y = lax.rem(self.y + hop_order(i % 4), 4)
        return self.shard(x, 1 - self.h, y)

    def near(self, i):
        x = lax.rem(self.x + hop_order(i // 4), 4)
        y = lax.rem(self.y + hop_order(i % 4), 4)
        return self.shard(x, self.h, y)


def greet(p):
    barrier = pltpu.get_barrier_semaphore()

    def signal(s, r):
        pl.semaphore_signal(barrier, inc=1, device_id=(s, r), device_id_type=MESH)

    def near(i, _):
        signal(p.near(i), p.r)
        return 0

    def across(i, _):
        for r in range(4):
            signal(p.far(i), 4 * p.c + r)
        return 0

    @pl.when(p.hop == 0)
    def _():
        lax.fori_loop(0, 16, across, 0)

    lax.fori_loop(1, 16, near, 0)
    signal(p.s, p.partner)

    @pl.when(p.hop > 0)
    def _():
        signal(p.s, p.before)


def await_greetings(p):
    pl.semaphore_wait(pltpu.get_barrier_semaphore(), 15 + 16 + 1 + 1 - p.hop // 3)


class Exchange:
    def __init__(self, p, src, far_src, dst, direct, relayed, pair_direct, pair_relayed, sends):
        self.p, self.src, self.far_src, self.dst = p, src, far_src, dst
        self.direct, self.relayed = direct, relayed
        self.pair_direct, self.pair_relayed = pair_direct, pair_relayed
        self.sends = sends

    def send(self, src, dst, send_sem, recv_sem, s, r):
        pltpu.make_async_remote_copy(
            src_ref=src,
            dst_ref=dst,
            send_sem=self.sends.at[send_sem],
            recv_sem=recv_sem,
            device_id=(s, r),
            device_id_type=MESH,
        ).start()

    def send_across(self):
        p = self.p

        def one(i, _):
            to = p.far(i)
            into = self.dst.at[p.s, :, pl.ds(p.part, PART)]
            self.send(self.far_src.at[to], into, 0, self.relayed.at[p.s], to, p.first)
            return 0

        lax.fori_loop(0, 16, one, 0)

    def send_near(self):
        p = self.p
        into = self.dst.at[p.s, :, pl.ds(p.col, HALF)]

        def one(i, _):
            to = p.near(i)
            self.send(self.src.at[to], into, 1, self.direct.at[p.x], to, p.r)
            return 0

        pltpu.make_async_copy(self.src.at[p.s], into, self.direct.at[p.x]).start()
        lax.fori_loop(1, 16, one, 0)

    def far_band(self, k, col):
        slot = self.p.far(k)
        return self.dst.at[slot, :, pl.ds(col, HALF)], slot

    def near_bands(self, g, col):
        x = lax.rem(self.p.x + hop_order(g), 4)
        return self.dst.at[pl.ds(self.p.shard(x, self.p.h, 0), 4), :, pl.ds(col, HALF)], x

    def relay(self, k):
        p = self.p
        at, slot = self.far_band(k, p.col)
        pltpu.make_async_copy(at, at, self.relayed.at[slot]).wait()

        @pl.when(p.hop < 3)
        def _():
            self.send(at, at, 2, self.relayed.at[slot], p.s, p.after)

        self.send(at, at, 3, self.pair_relayed.at[slot], p.s, p.partner)

    def pass_near(self, g):
        p = self.p
        at, x = self.near_bands(g, p.col)
        pltpu.make_async_copy(at, at, self.direct.at[x]).wait()
        self.send(at, at, 4, self.pair_direct.at[x], p.s, p.partner)

    def gather(self):
        p = self.p

        def step(t, _):
            k = t - LAG * p.hop

            @pl.when((k >= 0) & (k < 16))
            def _():
                self.relay(k)

            @pl.when((t >= NEAR_AT) & (t < NEAR_AT + 4))
            def _():
                self.pass_near(t - NEAR_AT)

            return 0

        lax.fori_loop(0, 16 + 3 * LAG, step, 0)

        def partner_near(g, _):
            at, x = self.near_bands(g, p.other_col)
            pltpu.make_async_copy(at, at, self.pair_direct.at[x]).wait()
            return 0

        lax.fori_loop(0, 4, partner_near, 0)

        def partner_far(k, _):
            at, slot = self.far_band(k, p.other_col)
            pltpu.make_async_copy(at, at, self.pair_relayed.at[slot]).wait()
            return 0

        lax.fori_loop(0, 16, partner_far, 0)

    def finish_sends(self):
        p = self.p

        def drain(index, slots):
            of = self.src.at[pl.ds(0, slots)]
            pltpu.make_async_copy(of, of, self.sends.at[index]).wait()

        drain(0, 4)
        drain(1, 15)

        @pl.when(p.hop < 3)
        def _():
            drain(2, 16)

        drain(3, 16)
        drain(4, 16)


def halves(value, high_ref, low_ref):
    high = value.astype(BF16)
    high_ref[...] = high
    low_ref[...] = (value - high.astype(F32)).astype(BF16)


def mul(lh, ll, rh, rl):
    dot = functools.partial(jnp.dot, preferred_element_type=F32)
    return dot(lh[...], rh[...]) + (dot(lh[...], rl[...]) + dot(ll[...], rh[...]))


def chain(x_ref, gram, q, ah, al, rh, rl, ch, cl, qh, ql):
    eye = lax.broadcasted_iota(jnp.int32, (ROWS, ROWS), 0) == lax.broadcasted_iota(
        jnp.int32, (ROWS, ROWS), 1
    )
    values = x_ref[...].reshape(ROWS, COLS)
    raw = lax.dot_general(
        values, values, (((1,), (1,)), ((), ())), preferred_element_type=F32
    )
    gram[...] = raw
    square = jnp.sum(jnp.where(eye, raw, 0.0), axis=(0, 1), keepdims=True)
    inverse = 1.0 / (jnp.sqrt(square) + 1e-07)
    gram[...] = gram[...] * inverse * inverse
    q[...] = jnp.where(eye, 1.0, 0.0)
    halves(q[...], qh, ql)

    def sweep(i, _):
        halves(gram[...], ah, al)
        poly = coef_b * gram[...] + coef_c * mul(ah, al, ah, al)
        halves(poly, rh, rl)
        q[...] = coef_a * q[...] + mul(rh, rl, qh, ql)
        halves(q[...], qh, ql)

        @pl.when(i < ITERS - 1)
        def _():
            gram[...] = coef_a * gram[...] + mul(rh, rl, ah, al)
            halves(gram[...], ch, cl)
            gram[...] = coef_a * gram[...] + mul(ch, cl, rh, rl)

        return 0

    lax.fori_loop(0, ITERS, sweep, 0)
    return inverse * jnp.sqrt(F32(max(ROWS, COLS)))


def kernel(
    mom, grad, new_mom, update, mv, gv, nv, sb, sf, xb, yb, yf, ob,
    gram, q, ah, al, rh, rl, ch, cl, qh, ql,
    load_sem, store_sem, direct, relayed, pair_direct, pair_relayed, sends,
):
    p = Place()
    greet(p)

    def load(index, src, dst, col):
        return pltpu.make_async_copy(
            src.at[:, :, pl.ds(col, HALF)],
            dst.at[:, :, pl.ds(col, HALF)],
            load_sem.at[index],
        )

    loads = [
        load(0, mom, mv, p.col),
        load(1, grad, gv, p.col),
        load(2, mom, mv, p.other_col),
        load(3, grad, gv, p.other_col),
    ]
    for copy in loads:
        copy.start()
    loads[0].wait()
    loads[1].wait()

    def momentum(e, col):
        cols = pl.ds(col, HALF)
        g = gv[e, :, cols].astype(F32)
        n = (0.95 * mv[e, :, cols].astype(F32) + g).astype(BF16)
        nv[e, :, cols] = n
        return n, g

    def blend(e, _):
        n, g = momentum(e, p.col)
        sb[e] = (g + 0.95 * n.astype(F32)).astype(BF16)
        return 0

    def blend_far(e, _):
        cols = pl.ds(p.part, PART)
        g = gv[e, :, cols].astype(F32)
        n = (0.95 * mv[e, :, cols].astype(F32) + g).astype(BF16)
        sf[e] = (g + 0.95 * n.astype(F32)).astype(BF16)
        return 0

    lax.fori_loop(0, EXPERTS, blend, 0)
    loads[2].wait()
    loads[3].wait()
    lax.fori_loop(0, EXPERTS, blend_far, 0)
    await_greetings(p)

    def exchange(phase, src, far_src, dst):
        return Exchange(
            p, src, far_src, dst, direct.at[phase], relayed.at[phase],
            pair_direct.at[phase], pair_relayed.at[phase], sends.at[phase],
        )

    inward = exchange(0, sb, sf, xb)
    inward.send_across()
    inward.send_near()

    def rest(e, _):
        momentum(e, p.other_col)
        return 0

    lax.fori_loop(0, EXPERTS, rest, 0)
    store = pltpu.make_async_copy(nv, new_mom, store_sem.at[0])
    store.start()
    inward.gather()

    factor = chain(xb, gram, q, ah, al, rh, rl, ch, cl, qh, ql)

    dot = functools.partial(jnp.dot, preferred_element_type=F32)

    def product(h, cols, width):
        rows = [pl.ds(pl.multiple_of(x * 128 + h * 64, 64), 64) for x in range(4)]
        high = jnp.concatenate([qh[i, :] for i in rows], 0)
        low = jnp.concatenate([ql[i, :] for i in rows], 0)
        values = xb[:, :, pl.ds(cols, width)].reshape(ROWS, width)
        return ((dot(high, values) + dot(low, values)) * factor).astype(BF16)

    outward = exchange(1, yb, yf, ob)
    part = product(1 - p.h, p.part, PART).reshape(4, 4, BAND, PART)
    for x in range(4):
        yf[pl.ds(p.shard(x, 1 - p.h, 0), 4)] = part[x]
    outward.send_across()
    part = product(p.h, p.col, HALF).reshape(4, 4, BAND, HALF)
    for x in range(4):
        yb[pl.ds(p.shard(x, p.h, 0), 4)] = part[x]
    outward.send_near()
    outward.gather()
    out = pltpu.make_async_copy(ob, update, store_sem.at[1])
    out.start()
    inward.finish_sends()
    outward.finish_sends()
    store.wait()
    out.wait()


def shards(momentum, gradient):
    whole = (EXPERTS, BAND, COLS)
    dma = pltpu.SemaphoreType.DMA
    square = (ROWS, ROWS)
    return pl.pallas_call(
        kernel,
        out_shape=(
            jax.ShapeDtypeStruct(whole, BF16),
            jax.ShapeDtypeStruct(whole, BF16),
        ),
        in_specs=[pl.BlockSpec(memory_space=pl.ANY)] * 2,
        out_specs=[pl.BlockSpec(memory_space=pl.ANY)] * 2,
        scratch_shapes=[
            pltpu.VMEM(whole, BF16),
            pltpu.VMEM(whole, BF16),
            pltpu.VMEM(whole, BF16),
            pltpu.VMEM((EXPERTS, BAND, HALF), BF16),
            pltpu.VMEM((EXPERTS, BAND, PART), BF16),
            pltpu.VMEM(whole, BF16),
            pltpu.VMEM((EXPERTS, BAND, HALF), BF16),
            pltpu.VMEM((EXPERTS, BAND, PART), BF16),
            pltpu.VMEM(whole, BF16),
            pltpu.VMEM(square, F32),
            pltpu.VMEM(square, F32),
        ]
        + [pltpu.VMEM(square, BF16)] * 8
        + [
            dma((4,)),
            dma((2,)),
            dma((2, 4)),
            dma((2, 32)),
            dma((2, 4)),
            dma((2, 32)),
            dma((2, 5)),
        ],
        compiler_params=pltpu.CompilerParams(
            collective_id=0,
            has_side_effects=True,
            vmem_limit_bytes=48 * 1024 * 1024,
        ),
    )(momentum, gradient)


def solution(mesh):
    return jax.shard_map(
        shards,
        mesh=mesh,
        in_specs=(P(None, "shard", None), P(None, "shard", None)),
        out_specs=(P(None, "shard", None), P(None, "shard", None)),
        check_vma=False,
    )
```

time: 102 us -> 78.8 us (0.77)
  Pallas kernels: 98.8 us -> 75.4 us
    pallas_call x1, Pallas kernels: 98.8 us -> 75.4 us  [shards(): pl.pallas_call(kernel, out_shape=(jax.ShapeDtypeStruct(whole, BF16), jax....]
where the time goes in v2:
time: 78.8 us; the launch traced here: 78.7 us
  Pallas kernels  75.4 us (96%)
  local copies, waits for them, and re-layouts  2.64 us (3%)
    pallas_call x1, Pallas kernels, shards(): pl.pallas_call(kernel, out_shape=(jax.ShapeDtypeStruct(whole, BF16), jax....  75.4 us
    unnamed x2, local copies, waits for them, and re-layouts  2.64 us

profile of v2, /device:TPU:1, one launch (start us, length us, event | category | flops | bytes accessed | tf_op | source)
XLA Modules:
  0.0 78.7 jit_solution(10069149191959246931)
XLA Ops:
  0.6 75.4 %shard_map.41 = (bf16[32,16,2048]{2,1,0:T(8,128)(2,1)S(1)}, bf16[32,16,2048]{2,1,0:T(8,128)(2,1)S(1)}) custom-call(bf16[32,16,2048]{2,1,0:T(8,128)(2,1)} %mom.1, bf16[32,16,2048]{2,1,0:T(8,128)(2,1)} %grad.1), custom_call_target="tpu_custom_call" | custom-call | tf_op jit(solution)/shard_map/pallas_call | solution.py:360
  76.1 1.3 %copy.6 = bf16[32,16,2048]{2,1,0:T(8,128)(2,1)} copy(bf16[32,16,2048]{2,1,0:T(8,128)(2,1)S(1)} %get-tuple-element.4) | data formatting | bytes 4194304
  77.4 1.3 %copy.7 = bf16[32,16,2048]{2,1,0:T(8,128)(2,1)} copy(bf16[32,16,2048]{2,1,0:T(8,128)(2,1)S(1)} %get-tuple-element.5) | data formatting | bytes 4194304

commit v3 on v2

--- a/solution.py
+++ b/solution.py
@@ -44,6 +44,8 @@
         self.hop = (1 - self.c) * (3 - self.zl) + self.c * self.zl
         self.before = self.r + 2 - 4 * self.c
         self.after = self.r - 2 + 4 * self.c
+        self.collector = 7 * (self.r // 4)
+        self.collects = (7 - self.r) // 7 + self.r // 7
         self.first = 6 - 5 * (self.zl // 2)
         self.col = pl.multiple_of(self.c * HALF, HALF)
         self.other_col = pl.multiple_of((1 - self.c) * HALF, HALF)
@@ -63,35 +65,48 @@
         return self.shard(x, self.h, y)
 
 
+def signal(semaphore, s, r):
+    pl.semaphore_signal(semaphore, inc=1, device_id=(s, r), device_id_type=MESH)
+
+
 def greet(p):
     barrier = pltpu.get_barrier_semaphore()
 
-    def signal(s, r):
-        pl.semaphore_signal(barrier, inc=1, device_id=(s, r), device_id_type=MESH)
-
     def near(i, _):
-        signal(p.near(i), p.r)
+        signal(barrier, p.near(i), p.r)
         return 0
 
     def across(i, _):
-        for r in range(4):
-            signal(p.far(i), 4 * p.c + r)
+        signal(barrier, p.far(i), 7 * p.c)
         return 0
 
     @pl.when(p.hop == 0)
     def _():
         lax.fori_loop(0, 16, across, 0)
 
+    @pl.when(p.collects == 0)
+    def _():
+        signal(barrier, p.s, p.collector)
+
     lax.fori_loop(1, 16, near, 0)
-    signal(p.s, p.partner)
+    signal(barrier, p.s, p.partner)
 
     @pl.when(p.hop > 0)
     def _():
-        signal(p.s, p.before)
-
-
-def await_greetings(p):
-    pl.semaphore_wait(pltpu.get_barrier_semaphore(), 15 + 16 + 1 + 1 - p.hop // 3)
+        signal(barrier, p.s, p.before)
+
+
+def await_greetings(p, told):
+    pl.semaphore_wait(pltpu.get_barrier_semaphore(), 15 + 1 + 1 - p.hop // 3 + 19 * p.collects)
+
+    @pl.when(p.collects == 1)
+    def _():
+        for i in range(1, 4):
+            signal(told, p.s, p.collector + i - 2 * i * (p.r // 7))
+
+    @pl.when(p.collects == 0)
+    def _():
+        pl.semaphore_wait(told, 1)
 
 
 class Exchange:
@@ -209,101 +224,117 @@
         drain(4, 16)
 
 
-def halves(value, high_ref, low_ref):
-    high = value.astype(BF16)
-    high_ref[...] = high
-    low_ref[...] = (value - high.astype(F32)).astype(BF16)
-
-
-def mul(lh, ll, rh, rl):
+def chain(x_ref, gram, q, ah, al, rh, rl, ch, cl, qh, ql, q2h, q2l):
+    half = ROWS // 2
+    s0, s1, both = slice(0, half), slice(half, ROWS), slice(0, ROWS)
+    blocks = ((s0, s1), (s0, s0), (s1, s1))
     dot = functools.partial(jnp.dot, preferred_element_type=F32)
-    return dot(lh[...], rh[...]) + (dot(lh[...], rl[...]) + dot(ll[...], rh[...]))
-
-
-def chain(x_ref, gram, q, ah, al, rh, rl, ch, cl, qh, ql):
-    eye = lax.broadcasted_iota(jnp.int32, (ROWS, ROWS), 0) == lax.broadcasted_iota(
-        jnp.int32, (ROWS, ROWS), 1
-    )
+
+    def eye(rows, cols):
+        shape = (rows.stop - rows.start, cols.stop - cols.start)
+        row = lax.broadcasted_iota(jnp.int32, shape, 0) + rows.start
+        return row == lax.broadcasted_iota(jnp.int32, shape, 1) + cols.start
+
+    def put(value, rows, cols, pair):
+        def split(value, at):
+            high = value.astype(BF16)
+            pair[0][at] = high
+            pair[1][at] = (value - high.astype(F32)).astype(BF16)
+
+        split(value, (rows, cols))
+        if cols.stop > rows.stop:
+            split(value[:, half - cols.start :].T, (s1, s0))
+
+    def product(left, right, finish, into, keep=None):
+        for rows, cols in blocks:
+            a, b = left[0][rows, :], left[1][rows, :]
+            c, d = right[0][:, cols], right[1][:, cols]
+            value = finish(dot(a, c) + (dot(a, d) + dot(b, c)), rows, cols)
+            if keep is not None:
+                keep[rows, cols] = value
+            put(value, rows, cols, into)
+
+    def plus(ref):
+        return lambda value, rows, cols: coef_a * ref[rows, cols] + value
+
+    def poly(value, rows, cols):
+        return coef_b * gram[rows, cols] + coef_c * value
+
     values = x_ref[...].reshape(ROWS, COLS)
-    raw = lax.dot_general(
-        values, values, (((1,), (1,)), ((), ())), preferred_element_type=F32
-    )
-    gram[...] = raw
-    square = jnp.sum(jnp.where(eye, raw, 0.0), axis=(0, 1), keepdims=True)
+    nt = (((1,), (1,)), ((), ()))
+    square = 0.0
+    for rows, cols in blocks:
+        raw = lax.dot_general(values[rows], values[cols], nt, preferred_element_type=F32)
+        gram[rows, cols] = raw
+        if cols.start <= rows.start:
+            square += jnp.sum(jnp.where(eye(rows, cols), raw, 0.0), axis=(0, 1), keepdims=True)
     inverse = 1.0 / (jnp.sqrt(square) + 1e-07)
-    gram[...] = gram[...] * inverse * inverse
-    q[...] = jnp.where(eye, 1.0, 0.0)
-    halves(q[...], qh, ql)
-
-    def sweep(i, _):
-        halves(gram[...], ah, al)
-        poly = coef_b * gram[...] + coef_c * mul(ah, al, ah, al)
-        halves(poly, rh, rl)
-        q[...] = coef_a * q[...] + mul(rh, rl, qh, ql)
-        halves(q[...], qh, ql)
-
-        @pl.when(i < ITERS - 1)
-        def _():
-            gram[...] = coef_a * gram[...] + mul(rh, rl, ah, al)
-            halves(gram[...], ch, cl)
-            gram[...] = coef_a * gram[...] + mul(ch, cl, rh, rl)
-
-        return 0
-
-    lax.fori_loop(0, ITERS, sweep, 0)
+    A, R, C = (ah, al), (rh, rl), (ch, cl)
+    for rows, cols in blocks:
+        value = gram[rows, cols] * inverse * inverse
+        gram[rows, cols] = value
+        put(value, rows, cols, A)
+    now, later = (qh, ql), (q2h, q2l)
+    for i in range(ITERS):
+        if i == 0:
+            for rows, cols in blocks:
+                a, b = ah[rows, :], al[rows, :]
+                c, d = ah[:, cols], al[:, cols]
+                value = poly(dot(a, c) + (dot(a, d) + dot(b, c)), rows, cols)
+                put(value, rows, cols, R)
+                value = jnp.where(eye(rows, cols), coef_a, 0.0) + value
+                q[rows, cols] = value
+                put(value, rows, cols, now)
+        else:
+            product(A, A, poly, R)
+        if i < ITERS - 1:
+            product(R, A, plus(gram), C, gram)
+        if i > 0:
+            product(R, now, plus(q), later, q)
+            now, later = later, now
+        if i < ITERS - 1:
+            product(C, R, plus(gram), A, gram)
+
     return inverse * jnp.sqrt(F32(max(ROWS, COLS)))
 
 
 def kernel(
-    mom, grad, new_mom, update, mv, gv, nv, sb, sf, xb, yb, yf, ob,
-    gram, q, ah, al, rh, rl, ch, cl, qh, ql,
-    load_sem, store_sem, direct, relayed, pair_direct, pair_relayed, sends,
+    mom, grad, new_mom, update, mv, gv, sb, sf, xb, yb, yf,
+    gram, q, ah, al, rh, rl, ch, cl, qh, ql, q2h, q2l,
+    load_sem, told, direct, relayed, pair_direct, pair_relayed, sends,
 ):
     p = Place()
-    greet(p)
-
-    def load(index, src, dst, col):
-        return pltpu.make_async_copy(
-            src.at[:, :, pl.ds(col, HALF)],
-            dst.at[:, :, pl.ds(col, HALF)],
-            load_sem.at[index],
-        )
-
     loads = [
-        load(0, mom, mv, p.col),
-        load(1, grad, gv, p.col),
-        load(2, mom, mv, p.other_col),
-        load(3, grad, gv, p.other_col),
+        pltpu.make_async_copy(src, dst, load_sem.at[i])
+        for i, (src, dst) in enumerate(((mom, mv), (grad, gv)))
     ]
     for copy in loads:
         copy.start()
-    loads[0].wait()
-    loads[1].wait()
-
-    def momentum(e, col):
-        cols = pl.ds(col, HALF)
+    greet(p)
+    for copy in loads:
+        copy.wait()
+
+    def momentum(e, cols):
         g = gv[e, :, cols].astype(F32)
-        n = (0.95 * mv[e, :, cols].astype(F32) + g).astype(BF16)
-        nv[e, :, cols] = n
-        return n, g
-
-    def blend(e, _):
-        n, g = momentum(e, p.col)
-        sb[e] = (g + 0.95 * n.astype(F32)).astype(BF16)
+        return (0.95 * mv[e, :, cols].astype(F32) + g).astype(BF16), g
+
+    def blend(e, cols):
+        n, g = momentum(e, cols)
+        return (g + 0.95 * n.astype(F32)).astype(BF16)
+
+    def blend_far(i, _):
+        e = p.far(i)
+        sf[e] = blend(e, pl.ds(p.part, PART))
         return 0
 
-    def blend_far(e, _):
-        cols = pl.ds(p.part, PART)
-        g = gv[e, :, cols].astype(F32)
-        n = (0.95 * mv[e, :, cols].astype(F32) + g).astype(BF16)
-        sf[e] = (g + 0.95 * n.astype(F32)).astype(BF16)
+    def blend_near(i, _):
+        e = p.near(i)
+        sb[e] = blend(e, pl.ds(p.col, HALF))
         return 0
 
-    lax.fori_loop(0, EXPERTS, blend, 0)
-    loads[2].wait()
-    loads[3].wait()
-    lax.fori_loop(0, EXPERTS, blend_far, 0)
-    await_greetings(p)
+    lax.fori_loop(0, 16, blend_far, 0)
+    lax.fori_loop(0, 16, blend_near, 0)
+    await_greetings(p, told)
 
     def exchange(phase, src, far_src, dst):
         return Exchange(
@@ -315,16 +346,14 @@
     inward.send_across()
     inward.send_near()
 
-    def rest(e, _):
-        momentum(e, p.other_col)
+    def whole_momentum(e, _):
+        new_mom[e], _ = momentum(e, slice(None))
         return 0
 
-    lax.fori_loop(0, EXPERTS, rest, 0)
-    store = pltpu.make_async_copy(nv, new_mom, store_sem.at[0])
-    store.start()
+    lax.fori_loop(0, EXPERTS, whole_momentum, 0)
     inward.gather()
 
-    factor = chain(xb, gram, q, ah, al, rh, rl, ch, cl, qh, ql)
+    factor = chain(xb, gram, q, ah, al, rh, rl, ch, cl, qh, ql, q2h, q2l)
 
     dot = functools.partial(jnp.dot, preferred_element_type=F32)
 
@@ -335,7 +364,7 @@
         values = xb[:, :, pl.ds(cols, width)].reshape(ROWS, width)
         return ((dot(high, values) + dot(low, values)) * factor).astype(BF16)
 
-    outward = exchange(1, yb, yf, ob)
+    outward = exchange(1, yb, yf, update)
     part = product(1 - p.h, p.part, PART).reshape(4, 4, BAND, PART)
     for x in range(4):
         yf[pl.ds(p.shard(x, 1 - p.h, 0), 4)] = part[x]
@@ -345,12 +374,8 @@
         yb[pl.ds(p.shard(x, p.h, 0), 4)] = part[x]
     outward.send_near()
     outward.gather()
-    out = pltpu.make_async_copy(ob, update, store_sem.at[1])
-    out.start()
     inward.finish_sends()
     outward.finish_sends()
-    store.wait()
-    out.wait()
 
 
 def shards(momentum, gradient):
@@ -364,9 +389,8 @@
             jax.ShapeDtypeStruct(whole, BF16),
         ),
         in_specs=[pl.BlockSpec(memory_space=pl.ANY)] * 2,
-        out_specs=[pl.BlockSpec(memory_space=pl.ANY)] * 2,
+        out_specs=[pl.BlockSpec(memory_space=pltpu.VMEM)] * 2,
         scratch_shapes=[
-            pltpu.VMEM(whole, BF16),
             pltpu.VMEM(whole, BF16),
             pltpu.VMEM(whole, BF16),
             pltpu.VMEM((EXPERTS, BAND, HALF), BF16),
@@ -374,14 +398,13 @@
             pltpu.VMEM(whole, BF16),
             pltpu.VMEM((EXPERTS, BAND, HALF), BF16),
             pltpu.VMEM((EXPERTS, BAND, PART), BF16),
-            pltpu.VMEM(whole, BF16),
             pltpu.VMEM(square, F32),
             pltpu.VMEM(square, F32),
         ]
-        + [pltpu.VMEM(square, BF16)] * 8
+        + [pltpu.VMEM(square, BF16)] * 10
         + [
-            dma((4,)),
             dma((2,)),
+            pltpu.SemaphoreType.REGULAR,
             dma((2, 4)),
             dma((2, 32)),
             dma((2, 4)),

time: 78.8 us -> 72.8 us (0.924)
  Pallas kernels: 75.4 us -> 69.5 us
    pallas_call x1, Pallas kernels: 75.4 us -> 69.5 us  [shards(): pl.pallas_call(kernel, out_shape=(jax.ShapeDtypeStruct(whole, BF16), jax....]
where the time goes in v3:
time: 72.8 us; the launch traced here: 72.7 us
  Pallas kernels  69.5 us (95%)
  local copies, waits for them, and re-layouts  2.64 us (4%)
    pallas_call x1, Pallas kernels, shards(): pl.pallas_call(kernel, out_shape=(jax.ShapeDtypeStruct(whole, BF16), jax....  69.5 us
    unnamed x2, local copies, waits for them, and re-layouts  2.64 us

profile of v3, /device:TPU:1, one launch (start us, length us, event | category | flops | bytes accessed | tf_op | source)
XLA Modules:
  0.0 72.7 jit_solution(12346554091658858169)
XLA Ops:
  0.6 69.5 %shard_map.41 = (bf16[32,16,2048]{2,1,0:T(8,128)(2,1)S(1)}, bf16[32,16,2048]{2,1,0:T(8,128)(2,1)S(1)}) custom-call(bf16[32,16,2048]{2,1,0:T(8,128)(2,1)} %mom.1, bf16[32,16,2048]{2,1,0:T(8,128)(2,1)} %grad.1), custom_call_target="tpu_custom_call" | custom-call | tf_op jit(solution)/shard_map/pallas_call | solution.py:385
  70.1 1.3 %copy.6 = bf16[32,16,2048]{2,1,0:T(8,128)(2,1)} copy(bf16[32,16,2048]{2,1,0:T(8,128)(2,1)S(1)} %get-tuple-element.4) | data formatting | bytes 4194304
  71.4 1.3 %copy.7 = bf16[32,16,2048]{2,1,0:T(8,128)(2,1)} copy(bf16[32,16,2048]{2,1,0:T(8,128)(2,1)S(1)} %get-tuple-element.5) | data formatting | bytes 4194304

commit v4 on v3

--- a/solution.py
+++ b/solution.py
@@ -22,7 +22,7 @@
 
 BAND = ROWS // 32
 HALF = COLS // 2
-PART = COLS // 8
+PART = COLS // 4
 LAG = 4
 NEAR_AT = 13
 
@@ -44,24 +44,26 @@
         self.hop = (1 - self.c) * (3 - self.zl) + self.c * self.zl
         self.before = self.r + 2 - 4 * self.c
         self.after = self.r - 2 + 4 * self.c
-        self.collector = 7 * (self.r // 4)
+        self.end = self.zl // 3
+        self.sends_far = (self.zl == 0) | (self.zl == 3)
         self.collects = (7 - self.r) // 7 + self.r // 7
-        self.first = 6 - 5 * (self.zl // 2)
+        self.first = 6 - 5 * self.end
         self.col = pl.multiple_of(self.c * HALF, HALF)
         self.other_col = pl.multiple_of((1 - self.c) * HALF, HALF)
-        self.part = pl.multiple_of(self.r * PART, PART)
+        self.part = pl.multiple_of(self.end * HALF + self.c * PART, PART)
 
     def shard(self, x, h, y):
         return x * 8 + h * 4 + y
 
+    def around(self, i):
+        return lax.rem(self.x + hop_order(i // 4), 4), lax.rem(self.y + hop_order(i % 4), 4)
+
     def far(self, i):
-        x = lax.rem(self.x + hop_order(i // 4), 4)
-        y = lax.rem(self.y + hop_order(i % 4), 4)
+        x, y = self.around(i)
         return self.shard(x, 1 - self.h, y)
 
     def near(self, i):
-        x = lax.rem(self.x + hop_order(i // 4), 4)
-        y = lax.rem(self.y + hop_order(i % 4), 4)
+        x, y = self.around(i)
         return self.shard(x, self.h, y)
 
 
@@ -84,10 +86,6 @@
     def _():
         lax.fori_loop(0, 16, across, 0)
 
-    @pl.when(p.collects == 0)
-    def _():
-        signal(barrier, p.s, p.collector)
-
     lax.fori_loop(1, 16, near, 0)
     signal(barrier, p.s, p.partner)
 
@@ -97,24 +95,27 @@
 
 
 def await_greetings(p, told):
-    pl.semaphore_wait(pltpu.get_barrier_semaphore(), 15 + 1 + 1 - p.hop // 3 + 19 * p.collects)
+    pl.semaphore_wait(pltpu.get_barrier_semaphore(), 15 + 1 + 1 - p.hop // 3 + 16 * p.collects)
 
     @pl.when(p.collects == 1)
     def _():
-        for i in range(1, 4):
-            signal(told, p.s, p.collector + i - 2 * i * (p.r // 7))
-
-    @pl.when(p.collects == 0)
+        signal(told, p.s, p.partner)
+
+    @pl.when(p.sends_far & (p.collects == 0))
     def _():
         pl.semaphore_wait(told, 1)
 
 
 class Exchange:
-    def __init__(self, p, src, far_src, dst, direct, relayed, pair_direct, pair_relayed, sends):
-        self.p, self.src, self.far_src, self.dst = p, src, far_src, dst
+    def __init__(self, p, near_first, src, far_src, dst, direct, relayed, pair_direct, pair_relayed, sends):
+        self.p, self.near_first = p, near_first
+        self.src, self.far_src, self.dst = src, far_src, dst
         self.direct, self.relayed = direct, relayed
         self.pair_direct, self.pair_relayed = pair_direct, pair_relayed
         self.sends = sends
+
+    def slot(self, x, h, y, far):
+        return 16 * far + x * 4 + y if self.near_first else self.p.shard(x, h, y)
 
     def send(self, src, dst, send_sem, recv_sem, s, r):
         pltpu.make_async_remote_copy(
@@ -128,45 +129,46 @@
 
     def send_across(self):
         p = self.p
+        into = self.dst.at[self.slot(p.x, p.h, p.y, 1), :, pl.ds(p.part, PART)]
 
         def one(i, _):
-            to = p.far(i)
-            into = self.dst.at[p.s, :, pl.ds(p.part, PART)]
-            self.send(self.far_src.at[to], into, 0, self.relayed.at[p.s], to, p.first)
+            x, y = p.around(i)
+            done = self.relayed.at[p.x * 4 + p.y]
+            self.send(self.far_src.at[x * 4 + y], into, 0, done, p.far(i), p.first)
             return 0
 
         lax.fori_loop(0, 16, one, 0)
 
     def send_near(self):
         p = self.p
-        into = self.dst.at[p.s, :, pl.ds(p.col, HALF)]
+        into = self.dst.at[self.slot(p.x, p.h, p.y, 0), :, pl.ds(p.col, HALF)]
 
         def one(i, _):
-            to = p.near(i)
-            self.send(self.src.at[to], into, 1, self.direct.at[p.x], to, p.r)
+            x, y = p.around(i)
+            self.send(self.src.at[x * 4 + y], into, 1, self.direct.at[p.x], p.near(i), p.r)
             return 0
 
-        pltpu.make_async_copy(self.src.at[p.s], into, self.direct.at[p.x]).start()
+        pltpu.make_async_copy(self.src.at[p.x * 4 + p.y], into, self.direct.at[p.x]).start()
         lax.fori_loop(1, 16, one, 0)
 
     def far_band(self, k, col):
-        slot = self.p.far(k)
-        return self.dst.at[slot, :, pl.ds(col, HALF)], slot
+        x, y = self.p.around(k)
+        return self.dst.at[self.slot(x, 1 - self.p.h, y, 1), :, pl.ds(col, HALF)], x * 4 + y
 
     def near_bands(self, g, col):
         x = lax.rem(self.p.x + hop_order(g), 4)
-        return self.dst.at[pl.ds(self.p.shard(x, self.p.h, 0), 4), :, pl.ds(col, HALF)], x
+        return self.dst.at[pl.ds(self.slot(x, self.p.h, 0, 0), 4), :, pl.ds(col, HALF)], x
 
     def relay(self, k):
         p = self.p
-        at, slot = self.far_band(k, p.col)
-        pltpu.make_async_copy(at, at, self.relayed.at[slot]).wait()
+        at, band = self.far_band(k, p.col)
+        pltpu.make_async_copy(at, at, self.relayed.at[band]).wait()
 
         @pl.when(p.hop < 3)
         def _():
-            self.send(at, at, 2, self.relayed.at[slot], p.s, p.after)
-
-        self.send(at, at, 3, self.pair_relayed.at[slot], p.s, p.partner)
+            self.send(at, at, 2, self.relayed.at[band], p.s, p.after)
+
+        self.send(at, at, 3, self.pair_relayed.at[band], p.s, p.partner)
 
     def pass_near(self, g):
         p = self.p
@@ -174,7 +176,7 @@
         pltpu.make_async_copy(at, at, self.direct.at[x]).wait()
         self.send(at, at, 4, self.pair_direct.at[x], p.s, p.partner)
 
-    def gather(self):
+    def gather(self, with_near=lambda: None):
         p = self.p
 
         def step(t, _):
@@ -198,10 +200,11 @@
             return 0
 
         lax.fori_loop(0, 4, partner_near, 0)
+        with_near()
 
         def partner_far(k, _):
-            at, slot = self.far_band(k, p.other_col)
-            pltpu.make_async_copy(at, at, self.pair_relayed.at[slot]).wait()
+            at, band = self.far_band(k, p.other_col)
+            pltpu.make_async_copy(at, at, self.pair_relayed.at[band]).wait()
             return 0
 
         lax.fori_loop(0, 16, partner_far, 0)
@@ -213,7 +216,10 @@
             of = self.src.at[pl.ds(0, slots)]
             pltpu.make_async_copy(of, of, self.sends.at[index]).wait()
 
-        drain(0, 4)
+        @pl.when(p.sends_far)
+        def _():
+            drain(0, 8)
+
         drain(1, 15)
 
         @pl.when(p.hop < 3)
@@ -222,6 +228,14 @@
 
         drain(3, 16)
         drain(4, 16)
+
+
+def gram_block(x_ref, rows, cols):
+    left, right = (
+        x_ref[at.start // BAND : at.stop // BAND].reshape(ROWS // 2, COLS) for at in (rows, cols)
+    )
+    nt = (((1,), (1,)), ((), ()))
+    return lax.dot_general(left, right, nt, preferred_element_type=F32)
 
 
 def chain(x_ref, gram, q, ah, al, rh, rl, ch, cl, qh, ql, q2h, q2l):
@@ -260,14 +274,13 @@
     def poly(value, rows, cols):
         return coef_b * gram[rows, cols] + coef_c * value
 
-    values = x_ref[...].reshape(ROWS, COLS)
-    nt = (((1,), (1,)), ((), ()))
-    square = 0.0
     for rows, cols in blocks:
-        raw = lax.dot_general(values[rows], values[cols], nt, preferred_element_type=F32)
-        gram[rows, cols] = raw
-        if cols.start <= rows.start:
-            square += jnp.sum(jnp.where(eye(rows, cols), raw, 0.0), axis=(0, 1), keepdims=True)
+        if (rows, cols) != (s0, s0):
+            gram[rows, cols] = gram_block(x_ref, rows, cols)
+    square = sum(
+        jnp.sum(jnp.where(eye(rows, rows), gram[rows, rows], 0.0), axis=(0, 1), keepdims=True)
+        for rows in (s0, s1)
+    )
     inverse = 1.0 / (jnp.sqrt(square) + 1e-07)
     A, R, C = (ah, al), (rh, rl), (ch, cl)
     for rows, cols in blocks:
@@ -304,14 +317,20 @@
     load_sem, told, direct, relayed, pair_direct, pair_relayed, sends,
 ):
     p = Place()
-    loads = [
-        pltpu.make_async_copy(src, dst, load_sem.at[i])
-        for i, (src, dst) in enumerate(((mom, mv), (grad, gv)))
-    ]
-    for copy in loads:
-        copy.start()
+
+    def loads(j):
+        cols = pl.ds(pl.multiple_of(lax.rem(p.part + j * PART, COLS), PART), PART)
+        return [
+            pltpu.make_async_copy(src.at[:, :, cols], dst.at[:, :, cols], load_sem.at[2 * j + i])
+            for i, (src, dst) in enumerate(((mom, mv), (grad, gv)))
+        ]
+
+    pending = [loads(j) for j in range(4)]
+    for copies in pending:
+        for copy in copies:
+            copy.start()
     greet(p)
-    for copy in loads:
+    for copy in pending[0]:
         copy.wait()
 
     def momentum(e, cols):
@@ -323,27 +342,37 @@
         return (g + 0.95 * n.astype(F32)).astype(BF16)
 
     def blend_far(i, _):
-        e = p.far(i)
-        sf[e] = blend(e, pl.ds(p.part, PART))
+        x, y = p.around(i)
+        sf[x * 4 + y] = blend(p.far(i), pl.ds(p.part, PART))
         return 0
 
     def blend_near(i, _):
-        e = p.near(i)
-        sb[e] = blend(e, pl.ds(p.col, HALF))
+        x, y = p.around(i)
+        sb[x * 4 + y] = blend(p.near(i), pl.ds(p.col, HALF))
         return 0
-
-    lax.fori_loop(0, 16, blend_far, 0)
-    lax.fori_loop(0, 16, blend_near, 0)
-    await_greetings(p, told)
 
     def exchange(phase, src, far_src, dst):
         return Exchange(
-            p, src, far_src, dst, direct.at[phase], relayed.at[phase],
+            p, phase == 0, src, far_src, dst, direct.at[phase], relayed.at[phase],
             pair_direct.at[phase], pair_relayed.at[phase], sends.at[phase],
         )
 
     inward = exchange(0, sb, sf, xb)
-    inward.send_across()
+
+    @pl.when(p.sends_far)
+    def _():
+        lax.fori_loop(0, 16, blend_far, 0)
+
+    await_greetings(p, told)
+
+    @pl.when(p.sends_far)
+    def _():
+        inward.send_across()
+
+    for copies in pending[1:]:
+        for copy in copies:
+            copy.wait()
+    lax.fori_loop(0, 16, blend_near, 0)
     inward.send_near()
 
     def whole_momentum(e, _):
@@ -351,38 +380,55 @@
         return 0
 
     lax.fori_loop(0, EXPERTS, whole_momentum, 0)
-    inward.gather()
+
+    half = ROWS // 2
+    near_rows, far_rows = slice(0, half), slice(half, ROWS)
+
+    def near_gram():
+        gram[near_rows, near_rows] = gram_block(xb, near_rows, near_rows)
+
+    inward.gather(near_gram)
 
     factor = chain(xb, gram, q, ah, al, rh, rl, ch, cl, qh, ql, q2h, q2l)
 
     dot = functools.partial(jnp.dot, preferred_element_type=F32)
 
-    def product(h, cols, width):
-        rows = [pl.ds(pl.multiple_of(x * 128 + h * 64, 64), 64) for x in range(4)]
-        high = jnp.concatenate([qh[i, :] for i in rows], 0)
-        low = jnp.concatenate([ql[i, :] for i in rows], 0)
+    def product(rows, cols, width):
         values = xb[:, :, pl.ds(cols, width)].reshape(ROWS, width)
-        return ((dot(high, values) + dot(low, values)) * factor).astype(BF16)
+        out = (dot(qh[rows, :], values) + dot(ql[rows, :], values)) * factor
+        return out.astype(BF16).reshape(16, BAND, width)
 
     outward = exchange(1, yb, yf, update)
-    part = product(1 - p.h, p.part, PART).reshape(4, 4, BAND, PART)
-    for x in range(4):
-        yf[pl.ds(p.shard(x, 1 - p.h, 0), 4)] = part[x]
-    outward.send_across()
-    part = product(p.h, p.col, HALF).reshape(4, 4, BAND, HALF)
-    for x in range(4):
-        yb[pl.ds(p.shard(x, p.h, 0), 4)] = part[x]
+
+    @pl.when(p.sends_far)
+    def _():
+        yf[...] = product(far_rows, p.part, PART)
+        outward.send_across()
+
+    yb[...] = product(near_rows, p.col, HALF)
     outward.send_near()
     outward.gather()
     inward.finish_sends()
     outward.finish_sends()
 
 
+def write_out(first, second, first_out, second_out, sem):
+    copies = [
+        pltpu.make_async_copy(src.at[pl.ds(8 * j, 8)], dst.at[pl.ds(8 * j, 8)], sem.at[i, j])
+        for j in range(4)
+        for i, (src, dst) in enumerate(((first, first_out), (second, second_out)))
+    ]
+    for copy in copies:
+        copy.start()
+    for copy in copies:
+        copy.wait()
+
+
 def shards(momentum, gradient):
     whole = (EXPERTS, BAND, COLS)
     dma = pltpu.SemaphoreType.DMA
     square = (ROWS, ROWS)
-    return pl.pallas_call(
+    results = pl.pallas_call(
         kernel,
         out_shape=(
             jax.ShapeDtypeStruct(whole, BF16),
@@ -393,22 +439,22 @@
         scratch_shapes=[
             pltpu.VMEM(whole, BF16),
             pltpu.VMEM(whole, BF16),
-            pltpu.VMEM((EXPERTS, BAND, HALF), BF16),
-            pltpu.VMEM((EXPERTS, BAND, PART), BF16),
+            pltpu.VMEM((16, BAND, HALF), BF16),
+            pltpu.VMEM((16, BAND, PART), BF16),
             pltpu.VMEM(whole, BF16),
-            pltpu.VMEM((EXPERTS, BAND, HALF), BF16),
-            pltpu.VMEM((EXPERTS, BAND, PART), BF16),
+            pltpu.VMEM((16, BAND, HALF), BF16),
+            pltpu.VMEM((16, BAND, PART), BF16),
             pltpu.VMEM(square, F32),
             pltpu.VMEM(square, F32),
         ]
         + [pltpu.VMEM(square, BF16)] * 10
         + [
-            dma((2,)),
+            dma((8,)),
             pltpu.SemaphoreType.REGULAR,
             dma((2, 4)),
-            dma((2, 32)),
+            dma((2, 16)),
             dma((2, 4)),
-            dma((2, 32)),
+            dma((2, 16)),
             dma((2, 5)),
         ],
         compiler_params=pltpu.CompilerParams(
@@ -417,6 +463,17 @@
             vmem_limit_bytes=48 * 1024 * 1024,
         ),
     )(momentum, gradient)
+    return pl.pallas_call(
+        write_out,
+        out_shape=(
+            jax.ShapeDtypeStruct(whole, BF16),
+            jax.ShapeDtypeStruct(whole, BF16),
+        ),
+        in_specs=[pl.BlockSpec(memory_space=pl.ANY)] * 2,
+        out_specs=[pl.BlockSpec(memory_space=pltpu.HBM)] * 2,
+        scratch_shapes=[dma((2, 4))],
+        compiler_params=pltpu.CompilerParams(vmem_limit_bytes=1024 * 1024),
+    )(*results)
 
 
 def solution(mesh):

time: 72.8 us -> 72.6 us (level)
  local copies, waits for them, and re-layouts: 2.64 us -> 0 us
  Pallas kernels: 69.5 us -> 71.9 us
    unnamed x2 -> x0, local copies, waits for them, and re-layouts: 2.64 us -> none
    pallas_call x0 -> x1, Pallas kernels: none -> 2.07 us  [shards(): pl.pallas_call(write_out, out_shape=(jax.ShapeDtypeStruct(whole, BF16), j...]
where the time goes in v4:
time: 72.6 us; the launch traced here: 72.5 us
  Pallas kernels  71.9 us (99%)
    pallas_call x1, Pallas kernels, shards(): pl.pallas_call(kernel, out_shape=(jax.ShapeDtypeStruct(whole, BF16), jax....  69.8 us
    pallas_call x1, Pallas kernels, shards(): pl.pallas_call(write_out, out_shape=(jax.ShapeDtypeStruct(whole, BF16), j...  2.07 us

profile of v4, /device:TPU:1, one launch (start us, length us, event | category | flops | bytes accessed | tf_op | source)
XLA Modules:
  0.0 72.5 jit_solution(14400785560739501164)
XLA Ops:
  0.6 69.8 %shard_map.41 = (bf16[32,16,2048]{2,1,0:T(8,128)(2,1)S(1)}, bf16[32,16,2048]{2,1,0:T(8,128)(2,1)S(1)}) custom-call(bf16[32,16,2048]{2,1,0:T(8,128)(2,1)} %mom.1, bf16[32,16,2048]{2,1,0:T(8,128)(2,1)} %grad.1), custom_call_target="tpu_custom_call" | custom-call | tf_op jit(solution)/shard_map/pallas_call | solution.py:431
  70.5 2.1 %shard_map.42 = (bf16[32,16,2048]{2,1,0:T(8,128)(2,1)}, bf16[32,16,2048]{2,1,0:T(8,128)(2,1)}) custom-call(bf16[32,16,2048]{2,1,0:T(8,128)(2,1)S(1)} %get-tuple-element.4.first, bf16[32,16,2048]{2,1,0:T(8,128)(2,1)S(1)} %get-tuple-element.5.second), custom_call_target="tpu_custom_call" | custom-call | tf_op jit(solution)/shard_map/pallas_call | solution.py:466

commit v5 on v4

--- a/solution.py
+++ b/solution.py
@@ -24,7 +24,7 @@
 HALF = COLS // 2
 PART = COLS // 4
 LAG = 4
-NEAR_AT = 13
+NEAR_AT = 20
 
 
 def hop_order(step):

time: 72.6 us -> 72.6 us (level)
  no operation moved by 1% of the time
where the time goes in v5:
time: 72.6 us; the launch traced here: 72.5 us
  Pallas kernels  71.8 us (99%)
    pallas_call x1, Pallas kernels, shards(): pl.pallas_call(kernel, out_shape=(jax.ShapeDtypeStruct(whole, BF16), jax....  69.8 us
    pallas_call x1, Pallas kernels, shards(): pl.pallas_call(write_out, out_shape=(jax.ShapeDtypeStruct(whole, BF16), j...  2.07 us

profile of v5, /device:TPU:1, one launch (start us, length us, event | category | flops | bytes accessed | tf_op | source)
XLA Modules:
  0.0 72.5 jit_solution(9291335862511954039)
XLA Ops:
  0.6 69.8 %shard_map.41 = (bf16[32,16,2048]{2,1,0:T(8,128)(2,1)S(1)}, bf16[32,16,2048]{2,1,0:T(8,128)(2,1)S(1)}) custom-call(bf16[32,16,2048]{2,1,0:T(8,128)(2,1)} %mom.1, bf16[32,16,2048]{2,1,0:T(8,128)(2,1)} %grad.1), custom_call_target="tpu_custom_call" | custom-call | tf_op jit(solution)/shard_map/pallas_call | solution.py:431
  70.4 2.1 %shard_map.42 = (bf16[32,16,2048]{2,1,0:T(8,128)(2,1)}, bf16[32,16,2048]{2,1,0:T(8,128)(2,1)}) custom-call(bf16[32,16,2048]{2,1,0:T(8,128)(2,1)S(1)} %get-tuple-element.4.first, bf16[32,16,2048]{2,1,0:T(8,128)(2,1)S(1)} %get-tuple-element.5.second), custom_call_target="tpu_custom_call" | custom-call | tf_op jit(solution)/shard_map/pallas_call | solution.py:466
